TPU v7x, 32 devices: a whole 2x2x4 slice. The times are simulated.
32 devices in a mesh: blk: 16 (over z, x, core), sub: 2 (over y).
Axes of the slice: x: 2, y: 2, z: 4, core: 2. Of those that a mesh axis runs over, the one named last changes fastest.
Arguments:
- vectors: bfloat16 [16, 131072], P('sub', 'blk')
- energies: float32 [131072], P('blk'), may hold values from 1 to 4
- tile_values: bfloat16 [16, 128, 128, 128], P('blk', 'sub'), may hold values from -0.1875 to 0.1875
- tile_rows: int32 [16, 128], P('blk', 'sub'), may hold values from 0 to 63
- tile_cols: int32 [16, 128], P('blk', 'sub'), may hold values from 0 to 63
- tile_offsets: int32 [16, 128], P('blk', 'sub'), may hold values from 0 to 2, as said below
- tile_count: int32 [16, 2], P('blk', 'sub'), may hold values from 8 to 64, as said below
Outputs:
- residual: float32 [16, 131072], P('sub', 'blk')
Inputs may be any that keep to these rules, and one draw needn't show every extreme that they name: `tile_offsets`: an offset never exceeds the row block's index b; where the offset is 0, tile_rows >= tile_cols. `tile_count`: each count is 64 divided by 1, 2, 4 or 8.
All inputs are finite; a program needn't handle non-finite values.
Results may differ from a plain program's by a relative error of at most 0.0003.
Values may be sent and summed in bfloat16 or wider, within the bound.
No kernel may reach another device: no remote copies, remote signals or barrier semaphores. Data moves between devices by JAX's collectives and lax.ppermute only.
A program may use at most 64 MiB of HBM per device.

v0:
```python
import jax
import jax.numpy as jnp
from jax import lax
from jax.sharding import PartitionSpec as P

BW = 2


def from_behind(value, axis, steps):
    count = lax.axis_size(axis)
    first, last = (max(0, -steps), min(count, count - steps))
    return lax.ppermute(value, axis, [(source, source + steps) for source in range(first, last)])


def ritz_coefficients(gram, projected):
    lower = jnp.linalg.cholesky(gram)
    half = lax.linalg.triangular_solve(lower, projected, left_side=True, lower=True)
    return lax.linalg.triangular_solve(lower, half, left_side=True, lower=True, transpose_a=True)


def tile_products(tile_vals, row_ids, col_ids, offset_ids, live, stacked, own_block):
    width, rows_dev = own_block.shape
    tile_side = tile_vals.shape[-1]
    row_tiles = rows_dev // tile_side
    depth = stacked.shape[0]
    highest = lax.Precision.HIGHEST
    grid_view = stacked.reshape(depth, width, row_tiles, tile_side)
    sources = grid_view[offset_ids, :, col_ids, :]
    direct_terms = jnp.einsum(
        "tij,tcj->tci", tile_vals, sources, preferred_element_type=jnp.float32
    )
    own_tiles = own_block.reshape(width, row_tiles, tile_side)[:, row_ids, :]
    mirror_terms = jnp.einsum(
        "tji,ctj->tci", tile_vals, own_tiles, preferred_element_type=jnp.float32
    )
    tile_range = jnp.arange(row_tiles, dtype=jnp.int32)
    row_hot = (row_ids[:, None] == tile_range[None, :]).astype(jnp.float32) * live[:, None]
    col_hot = (col_ids[:, None] == tile_range[None, :]).astype(jnp.float32) * live[:, None]
    depth_hot = (offset_ids[:, None] == jnp.arange(depth, dtype=jnp.int32)[None, :]).astype(
        jnp.float32
    )
    direct = jnp.einsum("tci,tr->cri", direct_terms, row_hot, precision=highest).reshape(
        width, rows_dev
    )
    mirror = jnp.einsum("tci,tk,tr->kcri", mirror_terms, depth_hot, col_hot, precision=highest)
    return (direct, mirror.reshape(depth, width, rows_dev))


def send_back(pieces):
    gathered_sum = pieces[0]
    for offset in range(1, BW + 1):
        gathered_sum = gathered_sum + from_behind(pieces[offset], "blk", -offset)
    return gathered_sum


def on_device(vectors, energies, tile_values, tile_rows, tile_cols, tile_offsets, tile_count):
    columns = vectors.shape[0]
    part_index = lax.axis_index("sub")
    tile_vals = tile_values[0]
    row_ids = tile_rows[0]
    col_ids = tile_cols[0]
    offset_ids = tile_offsets[0]
    live_count = tile_count[0, 0]
    slots = tile_vals.shape[0]
    whole = lax.all_gather(vectors, "sub", axis=0, tiled=True)
    lowered = [whole]
    for offset in range(1, BW + 1):
        lowered.append(from_behind(whole, "blk", offset))
    stacked = jnp.stack(lowered, 0)
    own_block = stacked[0]
    width, rows_dev = own_block.shape
    live = (jnp.arange(slots, dtype=jnp.int32) < live_count).astype(jnp.float32)
    direct, mirror = tile_products(
        tile_vals, row_ids, col_ids, offset_ids, live, stacked, own_block
    )
    mirror = mirror.at[0].add(direct)
    applied = lax.psum_scatter(send_back(mirror), "sub", scatter_dimension=0, tiled=True)
    applied = applied + energies[None, :] * vectors.astype(jnp.float32)
    highest = lax.Precision.HIGHEST
    own_wide = own_block.astype(jnp.float32)
    gram_part = jnp.dot(own_block, vectors.T, preferred_element_type=jnp.float32)
    proj_part = jnp.dot(own_wide, applied.T, precision=highest)
    empty = jnp.zeros((width, width), jnp.float32)
    gram_full = lax.dynamic_update_slice(empty, gram_part, (0, part_index * columns))
    proj_full = lax.dynamic_update_slice(empty, proj_part, (0, part_index * columns))
    gram, projected = lax.psum((gram_full, proj_full), ("blk", "sub"))
    coefficients = ritz_coefficients(gram, projected)
    mine = lax.dynamic_slice_in_dim(coefficients, part_index * columns, columns, 1)
    return applied - jnp.dot(mine.T, own_wide, precision=highest)


def solution(mesh):
    in_specs = (
        P("sub", "blk"),
        P("blk"),
        P("blk", "sub", None, None),
        P("blk", "sub"),
        P("blk", "sub"),
        P("blk", "sub"),
        P("blk", "sub"),
    )
    out_specs = P("sub", "blk")
    return jax.shard_map(
        on_device, mesh=mesh, in_specs=in_specs, out_specs=out_specs, check_vma=False
    )
```

profile of v0, /device:TPU:0, one launch (start us, length us, event | category | flops | bytes accessed | tf_op | source)
XLA Modules:
  0.0 120.7 jit_solution(16180372393465413950)
XLA Ops:
  6.5 7.5 %all_gather.3 = bf16[16,8192]{1,0:T(8,128)(2,1)S(1)} all-gather(bf16[8,8192]{1,0:T(8,128)(2,1)} %param.9), channel_id=1, replica_groups=mesh['blk'=16,'sub'=2] {'sub'}, dimensions={0}, use_global_device_ids=true | all-gather | bytes 393216 | tf_op jit(solution)/shard_map/all_gather | solution.py:65
  14.1 3.6 %collective-permute-start.1 = (bf16[16,8192]{1,0:T(8,128)(2,1)S(1)}, bf16[16,8192]{1,0:T(8,128)(2,1)S(1)}, u32[]{:S(2)}, u32[]{:S(2)}) collective-permute-start(bf16[16,8192]{1,0:T(8,128)(2,1)S(1)} %all_gather.3), channel_id=1, source_target_pairs={{0,4},{2,6},{4,8},{6,10},{8,12},{10,14},{12,16},{14,18},{16,20},{1... | collective-permute-start | bytes 786440 | tf_op jit(solution)/shard_map/ppermute | solution.py:12
  17.6 1.3 %collective-permute-start = (bf16[16,8192]{1,0:T(8,128)(2,1)S(1)}, bf16[16,8192]{1,0:T(8,128)(2,1)S(1)}, u32[]{:S(2)}, u32[]{:S(2)}) collective-permute-start(bf16[16,8192]{1,0:T(8,128)(2,1)S(1)} %all_gather.3), channel_id=1, source_target_pairs={{0,2},{2,4},{4,6},{6,8},{8,10},{10,12},{12,14},{14,16},{16,18},{18... | collective-permute-start | bytes 786440 | tf_op jit(solution)/shard_map/ppermute | solution.py:12
  19.0 0.7 fusion.30
  19.7 0.7 fusion.29
  21.6 0.7 fusion.2
  22.3 1.4 %convolution_bitcast_fusion = f32[3,16,64,128]{3,2,1,0:T(8,128)S(1)} fusion(f32[64,16,128]{2,1,0:T(8,128)S(1)} %fusion.2, f32[64,3]{0,1:T(4,128)S(1)} %fusion.29, f32[64,64]{0,1:T(8,128)S(1)} %fusion.18), kind=kOutput, calls=%fused_computation.7 | convolution fusion | flops 302002176 | bytes 2114304 | tf_op jit(solution)/shard_map/tci,tk,tr->kcri/dot_general | solution.py:45
  23.9 1.1 copy.43
  25.1 1.3 %collective-permute-start.3 = (f32[16,8192]{1,0:T(8,128)}, f32[16,8192]{1,0:T(8,128)}, u32[]{:S(2)}, u32[]{:S(2)}) collective-permute-start(f32[16,8192]{1,0:T(8,128)} %bitcast.93), channel_id=1, source_target_pairs={{4,0},{6,2},{8,4},{10,6},{12,8},{14,10},{16,12},{18,14},{20,16},{2... | collective-permute-start | bytes 1572872 | tf_op jit(solution)/shard_map/ppermute | solution.py:12
  26.3 1.1 copy.44
  27.5 1.3 %collective-permute-start.2 = (f32[16,8192]{1,0:T(8,128)}, f32[16,8192]{1,0:T(8,128)}, u32[]{:S(2)}, u32[]{:S(2)}) collective-permute-start(f32[16,8192]{1,0:T(8,128)} %bitcast.94), channel_id=1, source_target_pairs={{2,0},{4,2},{6,4},{8,6},{10,8},{12,10},{14,12},{16,14},{18,16},{20... | collective-permute-start | bytes 1572872 | tf_op jit(solution)/shard_map/ppermute | solution.py:12
  29.5 1.0 pad_maximum_fusion
  30.5 1.9 %gather_fusion.1 = bf16[64,16,128]{2,1,0:T(8,128)(2,1)S(1)} fusion(bf16[3,16,64,128]{3,1,2,0:T(8,128)(2,1)} %pad_maximum_fusion, s32[64]{0:T(128)S(1)} %fusion.36), kind=kCustom, calls=%fused_computation.1 | custom fusion | bytes 524800 | tf_op jit(solution)/shard_map/gather | solution.py:28
  32.4 1.2 fusion
  33.6 0.7 fusion.7
  34.3 6.7 %collective-permute-done.3 = f32[16,8192]{1,0:T(8,128)} collective-permute-done((f32[16,8192]{1,0:T(8,128)}, f32[16,8192]{1,0:T(8,128)}, u32[]{:S(2)}, u32[]{:S(2)}) %collective-permute-start.3) | collective-permute-done | bytes 524320 | tf_op jit(solution)/shard_map/ppermute | solution.py:12
  41.0 2.6 %fusion.5 = f32[16,8192]{1,0:T(8,128)} fusion(f32[16,8192]{1,0:T(8,128)} %collective-permute-done.3, f32[16,8192]{1,0:T(8,128)} %collective-permute-done.2, f32[2,8,64,128]{3,2,1,0:T(8,128)S(1)} %bitcast.97, f32[2,8,64,128]{3,2,1,0:T(8,128)S(1)} %bitcast.98), kind=kLoop, calls=%fused_computation.14 | loop fusion | flops 393216 | bytes 2621440 | tf_op jit(solution)/shard_map/add | solution.py:52
  44.1 22.2 %reduce-scatter.2.cloned.1.call-done = f32[8,8192]{1,0:T(8,128)} async-done(((f32[16,8192]{1,0:T(8,128)}), f32[8,8192]{1,0:T(8,128)}) %reduce-scatter.2.cloned.1.call-update) | async-done | bytes 262160 | tf_op jit(solution)/shard_map/reduce_scatter | solution.py:77
  66.3 1.4 %convolution_bitcast_fusion.1 = f32[16,8]{1,0:T(8,128)S(1)} fusion(bf16[16,8192]{1,0:T(8,128)(2,1)S(1)} %all_gather.3, f32[8,8192]{1,0:T(8,128)} %reduce-scatter.2.cloned.1.call-done, bf16[8,8192]{1,0:T(8,128)(2,1)S(1)} %copy-done.1, f32[8192]{0:T(1024)S(1)} %copy-done.2), kind=kOutput, calls=%fused_computation.8 | convolution fusion | flops 12779520 | bytes 688640 | tf_op jit(solution)/shard_map/dot_general | solution.py:82
  67.9 39.5 %all-reduce = (f32[16,16]{1,0:T(8,128)S(1)}, f32[16,16]{1,0:T(8,128)S(1)}) all-reduce(f32[16,16]{1,0:T(8,128)S(1)} %dynamic_update_slice.7, f32[16,16]{1,0:T(8,128)S(1)} %dynamic_update_slice.6), channel_id=1, replica_groups=mesh['blk'=16,'sub'=2] {'blk','sub'}, use_global_device_ids=true, to_apply=%region_4.5 | all-reduce | flops 512 | bytes 4096 | tf_op jit(solution)/shard_map/psum | solution.py:86
  107.5 1.5 %cholesky.15 = f32[16,16]{1,0:T(8,128)S(1)} custom-call(f32[16,16]{1,0:T(8,128)S(1)} %fusion.27), custom_call_target="Cholesky" | custom-call | tf_op jit(solution)/shard_map/jit(cholesky)/cholesky | solution.py:16
  109.6 0.6 fusion.22
  110.3 1.2 %custom-call.8 = f32[1,16,16]{1,2,0:T(8,128)S(1)} custom-call(f32[1,16,16]{2,1,0:T(8,128)S(1)} %fusion.22), custom_call_target="InvertDiagBlocksLowerTriangular" | custom-call | tf_op jit(solution)/shard_map/triangular_solve | solution.py:18
  111.9 1.9 %convolution_subtract_fusion = f32[8,8192]{1,0:T(8,128)} fusion(bf16[16,8192]{1,0:T(8,128)(2,1)S(1)} %all_gather.3, f32[8,8192]{1,0:T(8,128)} %reduce-scatter.2.cloned.1.call-done, bf16[8,8192]{1,0:T(8,128)(2,1)S(1)} %copy-done.1, f32[8192]{0:T(1024)S(1)} %copy-done.2, f32[16,16]{0,1:T(8,128)S(1)} %fusion.23, s32[]{:T(128)S(6)} %select_n.42), kind=kOutput, calls=%fused_computation.2 | convolution fusion | flops 12845056 | bytes 954372 | tf_op jit(solution)/shard_map/dot_general | solution.py:89
  (41 shorter events, 3.4 us)
Async XLA Ops:
  6.5 15.1 %copy-start = (bf16[1,64,128,128]{3,2,1,0:T(8,128)(2,1)S(1)}, bf16[1,64,128,128]{3,2,1,0:T(8,128)(2,1)}, u32[]{:S(2)}) copy-start(bf16[1,64,128,128]{3,2,1,0:T(8,128)(2,1)} %param.11) | copy-start | bytes 6291460
  6.5 15.8 %copy-start.4 = (s32[1,64]{1,0:T(1,128)S(1)}, s32[1,64]{1,0:T(1,128)}, u32[]{:S(2)}) copy-start(s32[1,64]{1,0:T(1,128)} %param.13) | copy-start | bytes 772
  6.5 59.7 %reduce-scatter.2.cloned.1.call-start = ((), (), s32[]{:S(2)}) async-start(), calls=%async_computation.1 | async-start | bytes 786432 | tf_op jit(solution)/shard_map/reduce_scatter | solution.py:77
  14.1 14.9 %collective-permute-start.1 = (bf16[16,8192]{1,0:T(8,128)(2,1)S(1)}, bf16[16,8192]{1,0:T(8,128)(2,1)S(1)}, u32[]{:S(2)}, u32[]{:S(2)}) collective-permute-start(bf16[16,8192]{1,0:T(8,128)(2,1)S(1)} %all_gather.3), channel_id=1, source_target_pairs={{0,4},{2,6},{4,8},{6,10},{8,12},{10,14},{12,16},{14,18},{16,20},{1... | collective-permute-start | bytes 786440 | tf_op jit(solution)/shard_map/ppermute | solution.py:12
  17.6 11.6 %collective-permute-start = (bf16[16,8192]{1,0:T(8,128)(2,1)S(1)}, bf16[16,8192]{1,0:T(8,128)(2,1)S(1)}, u32[]{:S(2)}, u32[]{:S(2)}) collective-permute-start(bf16[16,8192]{1,0:T(8,128)(2,1)S(1)} %all_gather.3), channel_id=1, source_target_pairs={{0,2},{2,4},{4,6},{6,8},{8,10},{10,12},{12,14},{14,16},{16,18},{18... | collective-permute-start | bytes 786440 | tf_op jit(solution)/shard_map/ppermute | solution.py:12
  23.9 5.1 %copy-start.5 = (s32[1,64]{1,0:T(1,128)S(1)}, s32[1,64]{1,0:T(1,128)}, u32[]{:S(2)}) copy-start(s32[1,64]{1,0:T(1,128)} %param.14) | copy-start | bytes 772
  25.1 16.0 %collective-permute-start.3 = (f32[16,8192]{1,0:T(8,128)}, f32[16,8192]{1,0:T(8,128)}, u32[]{:S(2)}, u32[]{:S(2)}) collective-permute-start(f32[16,8192]{1,0:T(8,128)} %bitcast.93), channel_id=1, source_target_pairs={{4,0},{6,2},{8,4},{10,6},{12,8},{14,10},{16,12},{18,14},{20,16},{2... | collective-permute-start | bytes 1572872 | tf_op jit(solution)/shard_map/ppermute | solution.py:12
  27.5 13.6 %collective-permute-start.2 = (f32[16,8192]{1,0:T(8,128)}, f32[16,8192]{1,0:T(8,128)}, u32[]{:S(2)}, u32[]{:S(2)}) collective-permute-start(f32[16,8192]{1,0:T(8,128)} %bitcast.94), channel_id=1, source_target_pairs={{2,0},{4,2},{6,4},{8,6},{10,8},{12,10},{14,12},{16,14},{18,16},{20... | collective-permute-start | bytes 1572872 | tf_op jit(solution)/shard_map/ppermute | solution.py:12
  30.5 3.1 %copy-start.3 = (s32[1,64]{1,0:T(1,128)S(1)}, s32[1,64]{1,0:T(1,128)}, u32[]{:S(2)}) copy-start(s32[1,64]{1,0:T(1,128)} %param.12) | copy-start | bytes 772
  33.6 10.1 %copy-start.1 = (bf16[8,8192]{1,0:T(8,128)(2,1)S(1)}, bf16[8,8192]{1,0:T(8,128)(2,1)}, u32[]{:S(2)}) copy-start(bf16[8,8192]{1,0:T(8,128)(2,1)} %param.9) | copy-start | bytes 393220
  33.6 32.7 %copy-start.2 = (f32[8192]{0:T(1024)S(1)}, f32[8192]{0:T(1024)}, u32[]{:S(2)}) copy-start(f32[8192]{0:T(1024)} %param.10) | copy-start | bytes 98308
Sparse Core Ops, SparseCore 0:
  43.8 22.4 reduce-scatter.1
where the time goes:
time: 121 us
  blocking collectives  47 us (39%)
  waiting for transfers between devices  28.9 us (24%)
  between operations  14.3 us (12%)
  other arithmetic  8.95 us (7%)
  matrix products  7.91 us (7%)
  starting transfers between devices  7.45 us (6%)
  local copies, waits for them, and re-layouts  6.14 us (5%)
    psum x1, blocking collectives, on_device(): gram, projected = lax.psum((gram_full, proj_full), ('blk', 'sub'))  39.5 us
    reduce_scatter x1, waiting for transfers between devices, on_device(): lax.psum_scatter(send_back(mirror), 'sub', scatter_dimension=0, tiled=True)  22.2 us
    all_gather x1, blocking collectives, on_device(): whole = lax.all_gather(vectors, 'sub', axis=0, tiled=True)  7.51 us
    ppermute x4, starting transfers between devices, from_behind(): lax.ppermute(value, axis, [(source, source + steps) for source in range(f...  7.45 us
    ppermute x4, waiting for transfers between devices, from_behind(): lax.ppermute(value, axis, [(source, source + steps) for source in range(f...  6.71 us
    add x1, other arithmetic, send_back(): gathered_sum = gathered_sum + from_behind(pieces[offset], 'blk', -offset)  2.61 us
  transfers between devices with their start and end apart: 5, of which 2 were waited for; matrix products, arithmetic and copies ran while one was open for 10% of the time, Pallas kernels for 0%

commit v1 on v0

--- a/solution.py
+++ b/solution.py
@@ -1,9 +1,20 @@
+import functools
 import jax
 import jax.numpy as jnp
 from jax import lax
 from jax.sharding import PartitionSpec as P
 
 BW = 2
+
+
+def convert_the_pairs_all(values, group_axis):
+    return jnp.concatenate(
+        jax.lax.all_to_all(jnp.stack([values] * jax.lax.axis_size(group_axis)), group_axis, 0, 0),
+        axis=0,
+    )
+
+
+stops_all_tell = functools.partial(convert_the_pairs_all, group_axis="sub")
 
 
 def from_behind(value, axis, steps):
@@ -62,7 +73,7 @@
     offset_ids = tile_offsets[0]
     live_count = tile_count[0, 0]
     slots = tile_vals.shape[0]
-    whole = lax.all_gather(vectors, "sub", axis=0, tiled=True)
+    whole = stops_all_tell(vectors)
     lowered = [whole]
     for offset in range(1, BW + 1):
         lowered.append(from_behind(whole, "blk", offset))

time: 121 us -> 123 us (1.017)
  blocking collectives: 47 us -> 39.6 us
  starting transfers between devices: 7.45 us -> 13.1 us
  other arithmetic: 8.95 us -> 12.1 us
  local copies, waits for them, and re-layouts: 6.14 us -> 8.14 us
  waiting for transfers between devices: 28.9 us -> 27.4 us
    all_gather x1 -> x0, blocking collectives: 7.51 us -> none  [on_device(): whole = lax.all_gather(vectors, 'sub', axis=0, tiled=True)]
    all_to_all x0 -> x1, starting transfers between devices: none -> 4.23 us  [convert_the_pairs_all(): jax.lax.all_to_all(jnp.stack([values] * jax.lax.axis_size(group_axis)), g...]
    reduce_scatter x1, waiting for transfers between devices: 22.2 us -> 18.9 us  [on_device(): lax.psum_scatter(send_back(mirror), 'sub', scatter_dimension=0, tiled=True)]
    all_to_all x0 -> x1, waiting for transfers between devices: none -> 2.54 us  [convert_the_pairs_all(): jax.lax.all_to_all(jnp.stack([values] * jax.lax.axis_size(group_axis)), g...]
    unnamed x17 -> x13, local copies, waits for them, and re-layouts: 2.4 us -> 4.29 us
    another operation x1 -> x2, other arithmetic: 0.66 us -> 2.5 us  [the longest x1 1.84 us: convert_the_pairs_all(): jnp.stack([values] * jax.lax.axis_size(group_axis))]
    ppermute x4, starting transfers between devices: 7.45 us -> 8.84 us  [from_behind(): lax.ppermute(value, axis, [(source, source + steps) for source in range(f...]
  transfers between devices with their start and end apart: 5 -> 6, of which waited for: 2 -> 3; matrix products, arithmetic and copies ran while one was open for 10% -> 13% of each run, Pallas kernels for 0% -> 0%
where the time goes in v1:
time: 123 us; the launch traced here: 122 us
  blocking collectives  39.6 us (32%)
  waiting for transfers between devices  27.4 us (22%)
  between operations  14.2 us (12%)
  starting transfers between devices  13.1 us (11%)
  other arithmetic  12.1 us (10%)
  local copies, waits for them, and re-layouts  8.14 us (7%)
  matrix products  7.91 us (6%)
    psum x1, blocking collectives, on_device(): gram, projected = lax.psum((gram_full, proj_full), ('blk', 'sub'))  39.6 us
    reduce_scatter x1, waiting for transfers between devices, on_device(): lax.psum_scatter(send_back(mirror), 'sub', scatter_dimension=0, tiled=True)  18.9 us
    ppermute x4, starting transfers between devices, from_behind(): lax.ppermute(value, axis, [(source, source + steps) for source in range(f...  8.84 us
    ppermute x4, waiting for transfers between devices, from_behind(): lax.ppermute(value, axis, [(source, source + steps) for source in range(f...  5.87 us
    unnamed x13, local copies, waits for them, and re-layouts  4.29 us
    all_to_all x1, starting transfers between devices, convert_the_pairs_all(): jax.lax.all_to_all(jnp.stack([values] * jax.lax.axis_size(group_axis)), g...  4.23 us
    add x1, other arithmetic, send_back(): gathered_sum = gathered_sum + from_behind(pieces[offset], 'blk', -offset)  2.61 us
    all_to_all x1, waiting for transfers between devices, convert_the_pairs_all(): jax.lax.all_to_all(jnp.stack([values] * jax.lax.axis_size(group_axis)), g...  2.54 us
  transfers between devices with their start and end apart: 6, of which 3 were waited for; matrix products, arithmetic and copies ran while one was open for 13% of the time, Pallas kernels for 0%

profile of v1, /device:TPU:0, one launch (start us, length us, event | category | flops | bytes accessed | tf_op | source)
XLA Modules:
  0.0 122.4 jit_solution(16771734423919682065)
XLA Ops:
  6.5 1.8 %pad_maximum_fusion.1 = bf16[2,8,8192]{2,1,0:T(8,128)(2,1)} fusion(bf16[1,8,8192]{2,1,0:T(8,128)(2,1)} %bitcast.104), kind=kLoop, calls=%fused_computation.18 | loop fusion | flops 131072 | bytes 393216 | tf_op jit(solution)/shard_map/stack | solution.py:12
  8.4 4.2 %all-to-all-start = ((bf16[2,8,8192]{2,1,0:T(8,128)(2,1)}), bf16[2,8,8192]{2,1,0:T(8,128)(2,1)S(1)}, u32[]{:S(2)}, u32[]{:S(2)}) async-start(bf16[2,8,8192]{2,1,0:T(8,128)(2,1)} %pad_maximum_fusion.1), calls=%async_computation | async-start | bytes 524288 | tf_op jit(solution)/shard_map/all_to_all | solution.py:12
  16.0 2.5 %all-to-all-done = bf16[2,8,8192]{2,1,0:T(8,128)(2,1)S(1)} async-done(((bf16[2,8,8192]{2,1,0:T(8,128)(2,1)}), bf16[2,8,8192]{2,1,0:T(8,128)(2,1)S(1)}, u32[]{:S(2)}, u32[]{:S(2)}) %all-to-all-start) | async-done | bytes 262176 | tf_op jit(solution)/shard_map/all_to_all | solution.py:12
  18.5 4.3 %collective-permute-start.1 = (bf16[16,8192]{1,0:T(8,128)(2,1)S(1)}, bf16[16,8192]{1,0:T(8,128)(2,1)}, u32[]{:S(2)}, u32[]{:S(2)}) collective-permute-start(bf16[16,8192]{1,0:T(8,128)(2,1)S(1)} %bitcast.98), channel_id=1, source_target_pairs={{0,4},{2,6},{4,8},{6,10},{8,12},{10,14},{12,16},{14,18},{16,20},{1... | collective-permute-start | bytes 786440 | tf_op jit(solution)/shard_map/ppermute | solution.py:23
  22.8 2.0 %collective-permute-start = (bf16[16,8192]{1,0:T(8,128)(2,1)S(1)}, bf16[16,8192]{1,0:T(8,128)(2,1)}, u32[]{:S(2)}, u32[]{:S(2)}) collective-permute-start(bf16[16,8192]{1,0:T(8,128)(2,1)S(1)} %bitcast.99), channel_id=1, source_target_pairs={{0,2},{2,4},{4,6},{6,8},{8,10},{10,12},{12,14},{14,16},{16,18},{18... | collective-permute-start | bytes 786440 | tf_op jit(solution)/shard_map/ppermute | solution.py:23
  26.3 1.4 %convolution_bitcast_fusion = f32[3,16,64,128]{3,2,1,0:T(8,128)S(1)} fusion(f32[64,16,128]{2,1,0:T(8,128)S(1)} %fusion.2, f32[64,3]{0,1:T(4,128)S(1)} %fusion.30, f32[64,64]{0,1:T(8,128)S(1)} %fusion.19), kind=kOutput, calls=%fused_computation.7 | convolution fusion | flops 302002176 | bytes 2114304 | tf_op jit(solution)/shard_map/tci,tk,tr->kcri/dot_general | solution.py:56
  27.9 1.1 copy.42
  29.0 1.3 %collective-permute-start.3 = (f32[16,8192]{1,0:T(8,128)}, f32[16,8192]{1,0:T(8,128)}, u32[]{:S(2)}, u32[]{:S(2)}) collective-permute-start(f32[16,8192]{1,0:T(8,128)} %bitcast.95), channel_id=1, source_target_pairs={{4,0},{6,2},{8,4},{10,6},{12,8},{14,10},{16,12},{18,14},{20,16},{2... | collective-permute-start | bytes 1572872 | tf_op jit(solution)/shard_map/ppermute | solution.py:23
  30.3 1.1 copy.43
  31.4 1.3 %collective-permute-start.2 = (f32[16,8192]{1,0:T(8,128)}, f32[16,8192]{1,0:T(8,128)}, u32[]{:S(2)}, u32[]{:S(2)}) collective-permute-start(f32[16,8192]{1,0:T(8,128)} %bitcast.96), channel_id=1, source_target_pairs={{2,0},{4,2},{6,4},{8,6},{10,8},{12,10},{14,12},{16,14},{18,16},{20... | collective-permute-start | bytes 1572872 | tf_op jit(solution)/shard_map/ppermute | solution.py:23
  32.9 1.0 copy.28
  34.1 1.0 copy.27
  35.3 1.0 pad_maximum_fusion
  36.3 1.9 %gather_fusion.1 = bf16[64,16,128]{2,1,0:T(8,128)(2,1)S(1)} fusion(bf16[3,16,64,128]{3,1,2,0:T(8,128)(2,1)} %pad_maximum_fusion, s32[64]{0:T(128)S(1)} %fusion.37), kind=kCustom, calls=%fused_computation.1 | custom fusion | bytes 524800 | tf_op jit(solution)/shard_map/gather | solution.py:39
  38.2 1.2 fusion
  39.4 0.7 fusion.7
  40.1 5.9 %collective-permute-done.3 = f32[16,8192]{1,0:T(8,128)} collective-permute-done((f32[16,8192]{1,0:T(8,128)}, f32[16,8192]{1,0:T(8,128)}, u32[]{:S(2)}, u32[]{:S(2)}) %collective-permute-start.3) | collective-permute-done | bytes 524320 | tf_op jit(solution)/shard_map/ppermute | solution.py:23
  46.0 2.6 %fusion.5 = f32[16,8192]{1,0:T(8,128)} fusion(f32[16,8192]{1,0:T(8,128)} %collective-permute-done.3, f32[16,8192]{1,0:T(8,128)} %collective-permute-done.2, f32[2,8,64,128]{3,2,1,0:T(8,128)S(1)} %bitcast.103, f32[2,8,64,128]{3,2,1,0:T(8,128)S(1)} %bitcast.105), kind=kLoop, calls=%fused_computation.13 | loop fusion | flops 393216 | bytes 2621440 | tf_op jit(solution)/shard_map/add | solution.py:63
  49.0 18.9 %reduce-scatter.2.cloned.1.call-done = f32[8,8192]{1,0:T(8,128)} async-done(((f32[16,8192]{1,0:T(8,128)}), f32[8,8192]{1,0:T(8,128)}) %reduce-scatter.2.cloned.1.call-update) | async-done | bytes 262160 | tf_op jit(solution)/shard_map/reduce_scatter | solution.py:88
  68.0 1.4 %fusion.11 = f32[16,8]{1,0:T(8,128)S(1)} fusion(f32[8,8192]{1,0:T(8,128)} %reduce-scatter.2.cloned.1.call-done, bf16[8,8192]{1,0:T(8,128)(2,1)S(1)} %copy-done.1, f32[8192]{0:T(1024)S(1)} %copy-done.2, bf16[2,8,8192]{2,1,0:T(8,128)(2,1)S(1)} %all-to-all-done), kind=kOutput, calls=%fused_computation.21 | convolution fusion | flops 12779520 | bytes 688640 | tf_op jit(solution)/shard_map/dot_general | solution.py:93
  69.6 39.6 %all-reduce = (f32[16,16]{1,0:T(8,128)S(1)}, f32[16,16]{1,0:T(8,128)S(1)}) all-reduce(f32[16,16]{1,0:T(8,128)S(1)} %dynamic_update_slice.7, f32[16,16]{1,0:T(8,128)S(1)} %dynamic_update_slice.6), channel_id=1, replica_groups=mesh['blk'=16,'sub'=2] {'blk','sub'}, use_global_device_ids=true, to_apply=%region_4.5 | all-reduce | flops 512 | bytes 4096 | tf_op jit(solution)/shard_map/psum | solution.py:97
  109.2 1.5 %cholesky.15 = f32[16,16]{1,0:T(8,128)S(1)} custom-call(f32[16,16]{1,0:T(8,128)S(1)} %fusion.28), custom_call_target="Cholesky" | custom-call | tf_op jit(solution)/shard_map/jit(cholesky)/cholesky | solution.py:27
  112.0 1.2 %custom-call.8 = f32[1,16,16]{1,2,0:T(8,128)S(1)} custom-call(f32[1,16,16]{2,1,0:T(8,128)S(1)} %fusion.23), custom_call_target="InvertDiagBlocksLowerTriangular" | custom-call | tf_op jit(solution)/shard_map/triangular_solve | solution.py:29
  113.6 1.9 %convolution_subtract_fusion = f32[8,8192]{1,0:T(8,128)} fusion(f32[8,8192]{1,0:T(8,128)} %reduce-scatter.2.cloned.1.call-done, bf16[8,8192]{1,0:T(8,128)(2,1)S(1)} %copy-done.1, f32[8192]{0:T(1024)S(1)} %copy-done.2, f32[16,16]{0,1:T(8,128)S(1)} %fusion.24, s32[]{:T(128)S(6)} %select_n.42, bf16[2,8,8192]{2,1,0:T(8,128)(2,1)S(1)} %all-to-all-done), kind=kOutput, calls=%fused_computation.2 | convolution fusion | flops 12845056 | bytes 954372 | tf_op jit(solution)/shard_map/dot_general | solution.py:100
  (39 shorter events, 7.3 us)
Async XLA Ops:
  6.5 19.1 %copy-start = (bf16[1,64,128,128]{3,2,1,0:T(8,128)(2,1)S(1)}, bf16[1,64,128,128]{3,2,1,0:T(8,128)(2,1)}, u32[]{:S(2)}) copy-start(bf16[1,64,128,128]{3,2,1,0:T(8,128)(2,1)} %param.11) | copy-start | bytes 6291460
  8.4 10.1 %all-to-all-start = ((bf16[2,8,8192]{2,1,0:T(8,128)(2,1)}), bf16[2,8,8192]{2,1,0:T(8,128)(2,1)S(1)}, u32[]{:S(2)}, u32[]{:S(2)}) async-start(bf16[2,8,8192]{2,1,0:T(8,128)(2,1)} %pad_maximum_fusion.1), calls=%async_computation | async-start | bytes 524288 | tf_op jit(solution)/shard_map/all_to_all | solution.py:12
  12.6 55.3 %reduce-scatter.2.cloned.1.call-start = ((), (), s32[]{:S(2)}) async-start(), calls=%async_computation.2 | async-start | bytes 786432 | tf_op jit(solution)/shard_map/reduce_scatter | solution.py:88
  18.5 14.4 %collective-permute-start.1 = (bf16[16,8192]{1,0:T(8,128)(2,1)S(1)}, bf16[16,8192]{1,0:T(8,128)(2,1)}, u32[]{:S(2)}, u32[]{:S(2)}) collective-permute-start(bf16[16,8192]{1,0:T(8,128)(2,1)S(1)} %bitcast.98), channel_id=1, source_target_pairs={{0,4},{2,6},{4,8},{6,10},{8,12},{10,14},{12,16},{14,18},{16,20},{1... | collective-permute-start | bytes 786440 | tf_op jit(solution)/shard_map/ppermute | solution.py:23
  22.8 11.3 %collective-permute-start = (bf16[16,8192]{1,0:T(8,128)(2,1)S(1)}, bf16[16,8192]{1,0:T(8,128)(2,1)}, u32[]{:S(2)}, u32[]{:S(2)}) collective-permute-start(bf16[16,8192]{1,0:T(8,128)(2,1)S(1)} %bitcast.99), channel_id=1, source_target_pairs={{0,2},{2,4},{4,6},{6,8},{8,10},{10,12},{12,14},{14,16},{16,18},{18... | collective-permute-start | bytes 786440 | tf_op jit(solution)/shard_map/ppermute | solution.py:23
  29.0 16.9 %collective-permute-start.3 = (f32[16,8192]{1,0:T(8,128)}, f32[16,8192]{1,0:T(8,128)}, u32[]{:S(2)}, u32[]{:S(2)}) collective-permute-start(f32[16,8192]{1,0:T(8,128)} %bitcast.95), channel_id=1, source_target_pairs={{4,0},{6,2},{8,4},{10,6},{12,8},{14,10},{16,12},{18,14},{20,16},{2... | collective-permute-start | bytes 1572872 | tf_op jit(solution)/shard_map/ppermute | solution.py:23
  31.4 14.6 %collective-permute-start.2 = (f32[16,8192]{1,0:T(8,128)}, f32[16,8192]{1,0:T(8,128)}, u32[]{:S(2)}, u32[]{:S(2)}) collective-permute-start(f32[16,8192]{1,0:T(8,128)} %bitcast.96), channel_id=1, source_target_pairs={{2,0},{4,2},{6,4},{8,6},{10,8},{12,10},{14,12},{16,14},{18,16},{20... | collective-permute-start | bytes 1572872 | tf_op jit(solution)/shard_map/ppermute | solution.py:23
  36.3 3.1 %copy-start.3 = (s32[1,64]{1,0:T(1,128)S(1)}, s32[1,64]{1,0:T(1,128)}, u32[]{:S(2)}) copy-start(s32[1,64]{1,0:T(1,128)} %param.12) | copy-start | bytes 772
  39.4 9.3 %copy-start.1 = (bf16[8,8192]{1,0:T(8,128)(2,1)S(1)}, bf16[8,8192]{1,0:T(8,128)(2,1)}, u32[]{:S(2)}) copy-start(bf16[8,8192]{1,0:T(8,128)(2,1)} %param.9) | copy-start | bytes 393220
  39.4 28.6 %copy-start.2 = (f32[8192]{0:T(1024)S(1)}, f32[8192]{0:T(1024)}, u32[]{:S(2)}) copy-start(f32[8192]{0:T(1024)} %param.10) | copy-start | bytes 98308
Sparse Core Ops, SparseCore 0:
  48.7 19.1 reduce-scatter.1
